TPU v7x, 512 devices: a whole 4x4x16 slice. The times are simulated.
512 devices in a mesh: seqhi: 16 (over z_lo, core), seqlo: 32 (over y, z_hi, x).
Axes of the slice: x: 4, y: 4, z: 16 (z_hi: 2, z_lo: 8; z = z_hi * 8 + z_lo), core: 2. Of those that a mesh axis runs over, the one named last changes fastest.
Arguments:
- features: float32 [131072, 256], P(('seqhi', 'seqlo')), may hold values from -6 to 6
- norm_gain: float32 [8, 512], replicated, may hold values from 0.1 to 1.9
- bias_hidden: float32 [8, 1024], replicated, may hold values from -4 to 4
- gate_logit: float32 [8, 512], replicated, may hold values from -2 to 2
- w_in: float32 [512, 1024], replicated, may hold values from -0.25 to 0.25
- w_out: float32 [1024, 512], replicated, may hold values from -0.1875 to 0.1875
Outputs:
- switched: float32 [131072, 256], P(('seqhi', 'seqlo'))
All inputs are finite; a program needn't handle non-finite values.
Results may differ from a plain program's by a relative error of at most 0.0001.
Values sent between devices are 32-bit elements; how exact they have to be, the bound alone decides.
A program may use at most 64 MiB of HBM per device.

v0:
```python
import jax
import jax.numpy as jnp
from jax import lax
from jax.sharding import PartitionSpec as P

HI_LAYERS = 4


NORM_EPS = 1e-05


def swapped(value, axis, apart):
    mask = 2**apart
    pairs = [(source, source ^ mask) for source in range(lax.axis_size(axis))]
    return lax.ppermute(value, axis, pairs)


def switch_unit(lower_rows, upper_rows, layer_params):
    norm_gain, bias_hidden, gate_logit, w_in, w_out = layer_params
    feature_count = lower_rows.shape[-1]
    paired = jnp.concatenate([lower_rows, upper_rows], axis=-1)
    center = paired - jnp.mean(paired, axis=-1, keepdims=True)
    spread = jnp.mean(center * center, axis=-1, keepdims=True)
    normed = center * lax.rsqrt(spread + NORM_EPS) * norm_gain
    hidden = jax.nn.gelu(
        jnp.dot(normed, w_in, precision=lax.Precision.HIGHEST, preferred_element_type=jnp.float32)
        + bias_hidden
    )
    mixed_out = jax.nn.sigmoid(gate_logit) * paired + jnp.dot(
        hidden, w_out, precision=lax.Precision.HIGHEST, preferred_element_type=jnp.float32
    )
    return (mixed_out[:, :feature_count], mixed_out[:, feature_count:])


def pair_layer(states, distance, layer_params):
    row_count, feature_count = states.shape
    groups = row_count // (2 * distance)
    grouped = states.reshape(groups, 2, distance, feature_count)
    new_lower, new_upper = switch_unit(
        grouped[:, 0].reshape(-1, feature_count),
        grouped[:, 1].reshape(-1, feature_count),
        layer_params,
    )
    joined = jnp.stack(
        [
            new_lower.reshape(groups, distance, feature_count),
            new_upper.reshape(groups, distance, feature_count),
        ],
        axis=1,
    )
    return joined.reshape(row_count, feature_count)


def high_partner(states, bit_index, layer_params):
    partner = swapped(states, "seqhi", bit_index)
    is_upper = lax.axis_index("seqhi") // 2**bit_index % 2 == 1
    lower_rows = jnp.where(is_upper, partner, states)
    upper_rows = jnp.where(is_upper, states, partner)
    new_lower, new_upper = switch_unit(lower_rows, upper_rows, layer_params)
    return jnp.where(is_upper, new_upper, new_lower)


def body(features, norm_gain, bias_hidden, gate_logit, w_in, w_out):
    local_rows = features.shape[0]
    high_count = lax.axis_size("seqhi")
    low_count = lax.axis_size("seqlo")
    high_bits = high_count.bit_length() - 1
    low_bits = low_count.bit_length() - 1
    layer_total = norm_gain.shape[0]
    high_layers = HI_LAYERS

    def params_of(layer_index):
        return (
            norm_gain[layer_index],
            bias_hidden[layer_index],
            gate_logit[layer_index],
            w_in,
            w_out,
        )

    states = features
    for layer_index in range(high_layers):
        states = high_partner(states, layer_index % high_bits, params_of(layer_index))
    low_states = states
    low_states = lax.all_to_all(low_states, "seqlo", split_axis=0, concat_axis=0, tiled=True)
    states = low_states
    for layer_index in range(high_layers, layer_total):
        distance = local_rows // low_count * 2 ** ((layer_index - high_layers) % low_bits)
        states = pair_layer(states, distance, params_of(layer_index))
    return lax.all_to_all(states, "seqlo", split_axis=0, concat_axis=0, tiled=True)


def solution(mesh):
    placed = (P(("seqhi", "seqlo"), None), P(), P(), P(), P(), P())
    return jax.shard_map(
        body, mesh=mesh, in_specs=placed, out_specs=P(("seqhi", "seqlo"), None), check_vma=False
    )
```

profile of v0, /device:TPU:1, one launch (start us, length us, event | category | flops | bytes accessed | tf_op | source)
XLA Modules:
  0.0 159.0 jit_solution(11653723594382761051)
XLA Ops:
  0.0 8.9 %collective-permute-start = (f32[256,256]{1,0:T(8,128)}, f32[256,256]{1,0:T(8,128)S(1)}, u32[]{:S(2)}, u32[]{:S(2)}) collective-permute-start(f32[256,256]{1,0:T(8,128)} %param.6), channel_id=1, source_target_pairs={{0,32},{32,0},{64,96},{96,64},{128,160},{160,128},{192,224},{224,1... | collective-permute-start | bytes 786440 | tf_op jit(solution)/shard_map/ppermute | solution.py:15
  13.4 2.1 %fusion.6 = f32[256,1024]{1,0:T(8,128)S(1)} fusion(f32[512,1024]{1,0:T(8,128)S(1)} %copy-done, f32[1024]{0:T(1024)S(1)} %bitcast.148, f32[256,256]{1,0:T(8,128)S(1)} %get-tuple-element.36, f32[256,256]{1,0:T(8,128)S(1)} %get-tuple-element.28, f32[512]{0:T(512)S(1)} %bitcast.152, f32[256]{0:T(256)S(1)} %add_rsqrt_fusion.3, f32[256]{0:T(256)S(1)} %add_multiply_fusion.7), kind=kOutput, calls=%fused_computation.22 | convolution fusion | flops 1613496320 | bytes 3678208 | tf_op jit(solution)/shard_map/dot_general | solution.py:26
  15.6 2.0 %multiply_add_fusion.3 = f32[256,512]{1,0:T(8,128)S(1)} fusion(f32[256,256]{1,0:T(8,128)S(1)} %get-tuple-element.36, f32[256,256]{1,0:T(8,128)S(1)} %get-tuple-element.28, f32[512]{0:T(512)S(1)} %bitcast.140, f32[256,1024]{1,0:T(8,128)S(1)} %fusion.6, f32[1024,512]{1,0:T(8,128)S(1)} %copy-done.1), kind=kOutput, calls=%fused_computation.95 | convolution fusion | flops 1611005952 | bytes 4196352 | tf_op jit(solution)/shard_map/dot_general | solution.py:29
  17.6 1.9 %collective-permute-start.1 = (f32[256,256]{1,0:T(8,128)S(1)}, f32[256,256]{1,0:T(8,128)S(1)}, u32[]{:S(2)}, u32[]{:S(2)}) collective-permute-start(f32[256,256]{1,0:T(8,128)S(1)} %slice_select_fusion.3), channel_id=1, source_target_pairs={{0,64},{32,96},{64,0},{96,32},{128,192},{160,224},{192,128},{224,1... | collective-permute-start | bytes 786440 | tf_op jit(solution)/shard_map/ppermute | solution.py:15
  19.5 7.8 %collective-permute-done.1 = f32[256,256]{1,0:T(8,128)S(1)} collective-permute-done((f32[256,256]{1,0:T(8,128)S(1)}, f32[256,256]{1,0:T(8,128)S(1)}, u32[]{:S(2)}, u32[]{:S(2)}) %collective-permute-start.1) | collective-permute-done | bytes 262176 | tf_op jit(solution)/shard_map/ppermute | solution.py:15
  27.7 2.1 %fusion.13 = f32[256,1024]{1,0:T(8,128)S(1)} fusion(f32[512,1024]{1,0:T(8,128)S(1)} %copy-done, f32[1024]{0:T(1024)S(1)} %bitcast.147, f32[256,256]{1,0:T(8,128)S(1)} %get-tuple-element.34, f32[256,256]{1,0:T(8,128)S(1)} %get-tuple-element.24, f32[512]{0:T(512)S(1)} %bitcast.151, f32[256]{0:T(256)S(1)} %add_rsqrt_fusion.2, f32[256]{0:T(256)S(1)} %add_multiply_fusion.6), kind=kOutput, calls=%fused_computation.29 | convolution fusion | flops 1613496320 | bytes 3678208 | tf_op jit(solution)/shard_map/dot_general | solution.py:26
  29.9 2.0 %multiply_add_fusion.2 = f32[256,512]{1,0:T(8,128)S(1)} fusion(f32[256,256]{1,0:T(8,128)S(1)} %get-tuple-element.34, f32[256,256]{1,0:T(8,128)S(1)} %get-tuple-element.24, f32[512]{0:T(512)S(1)} %bitcast.139, f32[256,1024]{1,0:T(8,128)S(1)} %fusion.13, f32[1024,512]{1,0:T(8,128)S(1)} %copy-done.2), kind=kOutput, calls=%fused_computation.91 | convolution fusion | flops 1611005952 | bytes 4196352 | tf_op jit(solution)/shard_map/dot_general | solution.py:29
  31.9 2.1 %collective-permute-start.2 = (f32[256,256]{1,0:T(8,128)S(1)}, f32[256,256]{1,0:T(8,128)S(1)}, u32[]{:S(2)}, u32[]{:S(2)}) collective-permute-start(f32[256,256]{1,0:T(8,128)S(1)} %slice_select_fusion.2), channel_id=1, source_target_pairs={{0,128},{32,160},{64,192},{96,224},{128,0},{160,32},{192,64},{224,... | collective-permute-start | bytes 786440 | tf_op jit(solution)/shard_map/ppermute | solution.py:15
  34.0 14.5 %collective-permute-done.2 = f32[256,256]{1,0:T(8,128)S(1)} collective-permute-done((f32[256,256]{1,0:T(8,128)S(1)}, f32[256,256]{1,0:T(8,128)S(1)}, u32[]{:S(2)}, u32[]{:S(2)}) %collective-permute-start.2) | collective-permute-done | bytes 262176 | tf_op jit(solution)/shard_map/ppermute | solution.py:15
  48.9 2.1 %fusion.20 = f32[256,1024]{1,0:T(8,128)S(1)} fusion(f32[512,1024]{1,0:T(8,128)S(1)} %copy-done, f32[1024]{0:T(1024)S(1)} %bitcast.146, f32[256,256]{1,0:T(8,128)S(1)} %get-tuple-element.32, f32[256,256]{1,0:T(8,128)S(1)} %get-tuple-element.20, f32[512]{0:T(512)S(1)} %bitcast.150, f32[256]{0:T(256)S(1)} %add_rsqrt_fusion.1, f32[256]{0:T(256)S(1)} %add_multiply_fusion.5), kind=kOutput, calls=%fused_computation.36 | convolution fusion | flops 1613496320 | bytes 3678208 | tf_op jit(solution)/shard_map/dot_general | solution.py:26
  51.0 2.0 %multiply_add_fusion.1 = f32[256,512]{1,0:T(8,128)S(1)} fusion(f32[256,256]{1,0:T(8,128)S(1)} %get-tuple-element.32, f32[256,256]{1,0:T(8,128)S(1)} %get-tuple-element.20, f32[512]{0:T(512)S(1)} %bitcast.138, f32[256,1024]{1,0:T(8,128)S(1)} %fusion.20, f32[1024,512]{1,0:T(8,128)S(1)} %copy-done.3), kind=kOutput, calls=%fused_computation.87 | convolution fusion | flops 1611005952 | bytes 4196352 | tf_op jit(solution)/shard_map/dot_general | solution.py:29
  53.0 3.7 %collective-permute-start.3 = (f32[256,256]{1,0:T(8,128)S(1)}, f32[256,256]{1,0:T(8,128)S(1)}, u32[]{:S(2)}, u32[]{:S(2)}) collective-permute-start(f32[256,256]{1,0:T(8,128)S(1)} %slice_select_fusion.1), channel_id=1, source_target_pairs={{0,256},{32,288},{64,320},{96,352},{128,384},{160,416},{192,448},{... | collective-permute-start | bytes 786440 | tf_op jit(solution)/shard_map/ppermute | solution.py:15
  56.8 24.5 %collective-permute-done.3 = f32[256,256]{1,0:T(8,128)S(1)} collective-permute-done((f32[256,256]{1,0:T(8,128)S(1)}, f32[256,256]{1,0:T(8,128)S(1)}, u32[]{:S(2)}, u32[]{:S(2)}) %collective-permute-start.3) | collective-permute-done | bytes 262176 | tf_op jit(solution)/shard_map/ppermute | solution.py:15
  81.7 2.1 %fusion.27 = f32[256,1024]{1,0:T(8,128)S(1)} fusion(f32[512,1024]{1,0:T(8,128)S(1)} %copy-done, f32[1024]{0:T(1024)S(1)} %bitcast.145, f32[256,256]{1,0:T(8,128)S(1)} %get-tuple-element.30, f32[256,256]{1,0:T(8,128)S(1)} %get-tuple-element.16, f32[512]{0:T(512)S(1)} %bitcast.149, f32[256]{0:T(256)S(1)} %add_rsqrt_fusion, f32[256]{0:T(256)S(1)} %add_multiply_fusion.4), kind=kOutput, calls=%fused_computation.43 | convolution fusion | flops 1613496320 | bytes 3678208 | tf_op jit(solution)/shard_map/dot_general | solution.py:26
  83.8 1.9 %multiply_add_fusion = f32[256,512]{1,0:T(8,128)S(1)} fusion(f32[256,256]{1,0:T(8,128)S(1)} %get-tuple-element.30, f32[256,256]{1,0:T(8,128)S(1)} %get-tuple-element.16, f32[512]{0:T(512)S(1)} %bitcast.137, f32[256,1024]{1,0:T(8,128)S(1)} %fusion.27, f32[1024,512]{1,0:T(8,128)S(1)} %copy-done.4), kind=kOutput, calls=%fused_computation.83 | convolution fusion | flops 1611005952 | bytes 4196352 | tf_op jit(solution)/shard_map/dot_general | solution.py:29
  85.8 32.2 %all_to_all.21 = f32[32,8,256]{2,1,0:T(8,128)S(1)} all-to-all(f32[32,8,256]{2,1,0:T(8,128)S(1)} %fusion.68), channel_id=1, replica_groups=mesh['seqhi'=16,'seqlo'=32] {'seqlo'}, dimensions={0} | all-to-all | bytes 524288 | tf_op jit(solution)/shard_map/all_to_all | solution.py:85
  118.5 1.4 fusion.34
  119.9 1.3 convolution_add_fusion.11
  121.6 1.4 fusion.41
  123.0 1.3 convolution_add_fusion.10
  124.8 1.4 fusion.48
  128.0 1.4 fusion.55
  129.4 1.3 convolution_add_fusion.8
  130.7 27.6 %all_to_all.22 = f32[32,8,256]{2,1,0:T(8,128)S(1)} all-to-all(f32[32,8,256]{2,1,0:T(8,128)S(1)} %bitcast.121), channel_id=1, replica_groups=mesh['seqhi'=16,'seqlo'=32] {'seqlo'}, dimensions={0} | all-to-all | bytes 524288 | tf_op jit(solution)/shard_map/all_to_all | solution.py:90
  (73 shorter events, 9.4 us)
Async XLA Ops:
  0.0 13.4 %copy-start = (f32[512,1024]{1,0:T(8,128)S(1)}, f32[512,1024]{1,0:T(8,128)}, u32[]{:S(2)}) copy-start(f32[512,1024]{1,0:T(8,128)} %param.10) | copy-start | bytes 6291460
  0.0 12.1 %collective-permute-start = (f32[256,256]{1,0:T(8,128)}, f32[256,256]{1,0:T(8,128)S(1)}, u32[]{:S(2)}, u32[]{:S(2)}) collective-permute-start(f32[256,256]{1,0:T(8,128)} %param.6), channel_id=1, source_target_pairs={{0,32},{32,0},{64,96},{96,64},{128,160},{160,128},{192,224},{224,1... | collective-permute-start | bytes 786440 | tf_op jit(solution)/shard_map/ppermute | solution.py:15
  13.4 2.2 %copy-start.1 = (f32[1024,512]{1,0:T(8,128)S(1)}, f32[1024,512]{1,0:T(8,128)}, u32[]{:S(2)}) copy-start(f32[1024,512]{1,0:T(8,128)} %param.11) | copy-start | bytes 6291460
  17.6 9.7 %collective-permute-start.1 = (f32[256,256]{1,0:T(8,128)S(1)}, f32[256,256]{1,0:T(8,128)S(1)}, u32[]{:S(2)}, u32[]{:S(2)}) collective-permute-start(f32[256,256]{1,0:T(8,128)S(1)} %slice_select_fusion.3), channel_id=1, source_target_pairs={{0,64},{32,96},{64,0},{96,32},{128,192},{160,224},{192,128},{224,1... | collective-permute-start | bytes 786440 | tf_op jit(solution)/shard_map/ppermute | solution.py:15
  27.7 2.2 %copy-start.2 = (f32[1024,512]{1,0:T(8,128)S(1)}, f32[1024,512]{1,0:T(8,128)}, u32[]{:S(2)}) copy-start(f32[1024,512]{1,0:T(8,128)} %param.11) | copy-start | bytes 6291460
  31.9 16.6 %collective-permute-start.2 = (f32[256,256]{1,0:T(8,128)S(1)}, f32[256,256]{1,0:T(8,128)S(1)}, u32[]{:S(2)}, u32[]{:S(2)}) collective-permute-start(f32[256,256]{1,0:T(8,128)S(1)} %slice_select_fusion.2), channel_id=1, source_target_pairs={{0,128},{32,160},{64,192},{96,224},{128,0},{160,32},{192,64},{224,... | collective-permute-start | bytes 786440 | tf_op jit(solution)/shard_map/ppermute | solution.py:15
  48.9 2.2 %copy-start.3 = (f32[1024,512]{1,0:T(8,128)S(1)}, f32[1024,512]{1,0:T(8,128)}, u32[]{:S(2)}) copy-start(f32[1024,512]{1,0:T(8,128)} %param.11) | copy-start | bytes 6291460
  53.0 28.3 %collective-permute-start.3 = (f32[256,256]{1,0:T(8,128)S(1)}, f32[256,256]{1,0:T(8,128)S(1)}, u32[]{:S(2)}, u32[]{:S(2)}) collective-permute-start(f32[256,256]{1,0:T(8,128)S(1)} %slice_select_fusion.1), channel_id=1, source_target_pairs={{0,256},{32,288},{64,320},{96,352},{128,384},{160,416},{192,448},{... | collective-permute-start | bytes 786440 | tf_op jit(solution)/shard_map/ppermute | solution.py:15
  81.7 2.2 %copy-start.4 = (f32[1024,512]{1,0:T(8,128)S(1)}, f32[1024,512]{1,0:T(8,128)}, u32[]{:S(2)}) copy-start(f32[1024,512]{1,0:T(8,128)} %param.11) | copy-start | bytes 6291460
  118.3 1.6 %copy-start.5 = (f32[1024,512]{1,0:T(8,128)S(1)}, f32[1024,512]{1,0:T(8,128)}, u32[]{:S(2)}) copy-start(f32[1024,512]{1,0:T(8,128)} %param.11) | copy-start | bytes 6291460
  121.4 1.6 %copy-start.6 = (f32[1024,512]{1,0:T(8,128)S(1)}, f32[1024,512]{1,0:T(8,128)}, u32[]{:S(2)}) copy-start(f32[1024,512]{1,0:T(8,128)} %param.11) | copy-start | bytes 6291460
  124.6 1.6 %copy-start.7 = (f32[1024,512]{1,0:T(8,128)S(1)}, f32[1024,512]{1,0:T(8,128)}, u32[]{:S(2)}) copy-start(f32[1024,512]{1,0:T(8,128)} %param.11) | copy-start | bytes 6291460
  127.8 1.6 %copy-start.8 = (f32[1024,512]{1,0:T(8,128)S(1)}, f32[1024,512]{1,0:T(8,128)}, u32[]{:S(2)}) copy-start(f32[1024,512]{1,0:T(8,128)} %param.11) | copy-start | bytes 6291460
where the time goes:
time: 160 us; the launch traced here: 159 us
  blocking collectives  59.7 us (37%)
  waiting for transfers between devices  46.8 us (29%)
  matrix products  27 us (17%)
  starting transfers between devices  16.6 us (10%)
  other arithmetic  4.88 us (3%)
  local copies, waits for them, and re-layouts  3.28 us (2%)
    ppermute x4, waiting for transfers between devices, swapped(): return lax.ppermute(value, axis, pairs)  46.8 us
    all_to_all x1, blocking collectives, body(): lax.all_to_all(low_states, 'seqlo', split_axis=0, concat_axis=0, tiled=True)  32.2 us
    all_to_all x1, blocking collectives, body(): lax.all_to_all(states, 'seqlo', split_axis=0, concat_axis=0, tiled=True)  27.6 us
    ppermute x4, starting transfers between devices, swapped(): return lax.ppermute(value, axis, pairs)  16.6 us
    dot_general x8, matrix products, switch_unit(): jnp.dot(normed, w_in, precision=lax.Precision.HIGHEST, preferred_element_...  14.1 us
    dot_general x8, matrix products, switch_unit(): jnp.dot(hidden, w_out, precision=lax.Precision.HIGHEST, preferred_element...  13 us
  transfers between devices with their start and end apart: 4, of which 3 were waited for; matrix products, arithmetic and copies ran while one was open for 2% of the time, Pallas kernels for 0%

commit v1 on v0

v1 whole, which is shorter than its diff:
```python
import functools

import jax
import jax.numpy as jnp
from jax import lax
from jax.experimental import pallas as pl
from jax.experimental.pallas import tpu as pltpu
from jax.sharding import PartitionSpec as P

MESH = pl.DeviceIdType.MESH
BF, F32 = jnp.bfloat16, jnp.float32
NORM_EPS = 1e-05
Z, ZLO, X, Y = 16, 8, 4, 2


def ring_order(size):
    order = []
    for step in range(size):
        half = (step + 1) // 2
        order.append((size // 2 - half if step % 2 else size // 2 + half) % size)
    return order


def chips(hi, lo):
    z_lo, x, z_hi, y = lax.div(hi, 2), lax.rem(lo, 4), lax.rem(lax.div(lo, 4), 2), lax.rem(lax.div(lo, 8), 2)
    block = lo - lax.rem(lo, 16)
    z = z_hi * ZLO + z_lo
    along_x = []
    for dx in (2, 1, 3, 0):
        to = lax.rem(x + dx, X)
        along_x.append((to, lax.rem(to, 2) * 8 + lax.div(to, 2) * 4))
    along_y = [1 - y, y]
    found = []
    for dz in ring_order(Z):
        to = lax.rem(z + dz, Z)
        to_hi, to_lo = lax.div(to, ZLO), lax.rem(to, ZLO)
        place_z = lax.rem(to_lo, 2) * 64 + lax.rem(lax.div(to_lo, 2), 2) * 32 + lax.div(to_lo, 4) * 16 + to_hi * 2
        at_z = block + to_hi * 4
        for to_x, place_x in along_x:
            for to_y in along_y:
                found.append((to_lo, at_z + to_x + to_y * 8, place_z + place_x + to_y))
    return found


def halves(value):
    high = value.astype(BF)
    return high, (value - high.astype(F32)).astype(BF)


def product(value, weight_high, weight_low):
    rows = value.shape[0]
    high, low = halves(value)
    both = jnp.dot(jnp.concatenate([high, low], 0), weight_high[...], preferred_element_type=F32)
    return both[:rows] + both[rows:] + jnp.dot(high, weight_low[...], preferred_element_type=F32)


def switch(lower, upper, layer, gain, bias, gate, w_in, w_out):
    wide = lower.shape[-1]
    mean = (jnp.sum(lower, -1, keepdims=True) + jnp.sum(upper, -1, keepdims=True)) * (0.5 / wide)
    lower_c, upper_c = lower - mean, upper - mean
    spread = (jnp.sum(lower_c * lower_c, -1, keepdims=True) + jnp.sum(upper_c * upper_c, -1, keepdims=True)) * (0.5 / wide)
    scale = lax.rsqrt(spread + NORM_EPS)
    normed = jnp.concatenate([lower_c * scale, upper_c * scale], -1) * gain[pl.ds(layer, 1), :]
    hidden = jax.nn.gelu(product(normed, *w_in) + bias[pl.ds(layer, 1), :])
    out = product(hidden, *w_out)
    kept = jax.nn.sigmoid(gate[pl.ds(layer, 1), :])
    return kept[:, :wide] * lower + out[:, :wide], kept[:, wide:] * upper + out[:, wide:]


def butterfly(points, params, layers):
    rows = points.shape[1] // 2

    def step(layer, carry):
        lower = jnp.concatenate([points[0, :rows], points[1, :rows]], -1)
        upper = jnp.concatenate([points[0, rows:], points[1, rows:]], -1)
        lower, upper = switch(lower, upper, layer, *params)
        for part in range(2):
            lanes = slice(part * 128, part * 128 + 128)
            points[part, pl.ds(0, rows, stride=2), :] = lower[:, lanes]
            points[part, pl.ds(1, rows, stride=2), :] = upper[:, lanes]
        return carry

    lax.fori_loop(1, layers, step, 0)


def split_weight(whole, high, low):
    rows = whole.shape[0]

    def step(index, carry):
        at = pl.ds(pl.multiple_of(index * 64, 64), 64)
        high[at, :], low[at, :] = halves(whole[at, :])
        return carry

    lax.fori_loop(0, rows // 64, step, 0)


def took(ref, sem):
    pltpu.make_async_copy(ref, ref, sem).wait()


def kernel(
    x_hbm, gain_hbm, bias_hbm, gate_hbm, w_in_hbm, w_out_hbm, out,
    gain, bias, gate, w_in, w_out, in_high, in_low, out_high, out_low,
    away, paired, mixed, points_a, points_b, spare, loads, core_sem, in_sem, out_sem,
):
    hi, lo = lax.axis_index("seqhi"), lax.axis_index("seqlo")
    core = lax.rem(hi, 2)
    other = 1 - core
    peers = chips(hi, lo)
    my_place = peers[-1][2]
    layers = gain.shape[0]
    half = paired.shape[1]

    barrier = pltpu.get_barrier_semaphore()
    for z_lo, to_lo, _ in peers[:-1]:
        pl.semaphore_signal(barrier, inc=1, device_id=(z_lo * 2 + core, to_lo), device_id_type=MESH)
    partner = (hi + 1 - 2 * core, lo)
    pl.semaphore_signal(barrier, inc=1, device_id=partner, device_id_type=MESH)

    keep_at = pl.ds(pl.multiple_of(core * half, half), half)
    send_at = pl.ds(pl.multiple_of(other * half, half), half)
    fetched = [
        pltpu.make_async_copy(source, target, loads.at[index])
        for index, (source, target) in enumerate(
            [
                (w_in_hbm, w_in), (w_out_hbm, w_out), (gain_hbm, gain), (bias_hbm, bias), (gate_hbm, gate),
                (x_hbm.at[send_at, :], away), (x_hbm.at[keep_at, :], paired.at[core]),
            ]
        )
    ]
    for copy in fetched:
        copy.start()
    fetched[0].wait()
    split_weight(w_in, in_high, in_low)
    fetched[1].wait()
    split_weight(w_out, out_high, out_low)
    for copy in fetched[2:]:
        copy.wait()
    params = (gain, bias, gate, (in_high, in_low), (out_high, out_low))

    pl.semaphore_wait(barrier, len(peers))
    swap = pltpu.make_async_remote_copy(
        src_ref=away, dst_ref=paired.at[core], send_sem=core_sem.at[0], recv_sem=core_sem.at[1],
        device_id=partner, device_id_type=MESH,
    )
    swap.start()
    swap.wait()
    lower, upper = switch(paired[0], paired[1], 0, *params)
    for part in range(2):
        lanes = slice(part * 128, part * 128 + 128)
        mixed[0, part] = lower[:, lanes]
        mixed[1, part] = upper[:, lanes]

    for which, points in enumerate((points_a, points_b)):
        whose = core if which == 0 else other
        for z_lo, to_lo, place in peers[:-1]:
            pltpu.make_async_remote_copy(
                src_ref=mixed.at[whose, :, pl.ds(place, 1), :], dst_ref=points.at[:, pl.ds(my_place, 1), :],
                send_sem=in_sem.at[0, which], recv_sem=in_sem.at[1, which],
                device_id=(z_lo * 2 + core, to_lo), device_id_type=MESH,
            ).start()
        own = mixed.at[whose, :, pl.ds(my_place, 1), :]
        pltpu.make_async_copy(own, points.at[:, pl.ds(my_place, 1), :], in_sem.at[1, which]).start()
        pltpu.make_async_copy(own, spare.at[which, :, pl.ds(0, 1), :], in_sem.at[0, which]).start()

    home = pl.ds(core * half + my_place, 1)
    for which, points in enumerate((points_a, points_b)):
        whose = core if which == 0 else other
        took(points, in_sem.at[1, which])
        butterfly(points, params, layers)
        for z_lo, to_lo, place in peers[: len(peers) - 1 + which]:
            for part in range(2):
                pltpu.make_async_remote_copy(
                    src_ref=points.at[part, pl.ds(place, 1), :], dst_ref=out.at[home, pl.ds(part * 128, 128)],
                    send_sem=out_sem.at[0, which], recv_sem=out_sem.at[1, which],
                    device_id=(z_lo * 2 + whose, to_lo), device_id_type=MESH,
                ).start()
        if which == 0:
            for part in range(2):
                own = points.at[part, pl.ds(my_place, 1), :]
                pltpu.make_async_copy(own, out.at[home, pl.ds(part * 128, 128)], out_sem.at[1, which]).start()
                pltpu.make_async_copy(own, spare.at[2, part, pl.ds(0, 1), :], out_sem.at[0, which]).start()

    for which, points in enumerate((points_a, points_b)):
        took(points, in_sem.at[0, which])
        took(points, out_sem.at[0, which])
    took(out.at[keep_at, :], out_sem.at[1, 0])
    took(out.at[send_at, :], out_sem.at[1, 1])


def body(features, norm_gain, bias_hidden, gate_logit, w_in, w_out):
    rows, wide = features.shape
    half = rows // 2
    anywhere = pl.BlockSpec(memory_space=pltpu.HBM)
    sem = pltpu.SemaphoreType.DMA
    vmem = lambda dtype, *shape: pltpu.VMEM(shape, dtype)
    return pl.pallas_call(
        kernel,
        out_shape=jax.ShapeDtypeStruct((rows, wide), F32),
        in_specs=[anywhere] * 6,
        out_specs=pl.BlockSpec(memory_space=pltpu.VMEM),
        scratch_shapes=[
            vmem(F32, *norm_gain.shape), vmem(F32, *bias_hidden.shape), vmem(F32, *gate_logit.shape),
            vmem(F32, *w_in.shape), vmem(F32, *w_out.shape),
            vmem(BF, *w_in.shape), vmem(BF, *w_in.shape), vmem(BF, *w_out.shape), vmem(BF, *w_out.shape),
            vmem(F32, half, wide), vmem(F32, 2, half, wide), vmem(F32, 2, 2, half, 128),
            vmem(F32, 2, half, 128), vmem(F32, 2, half, 128), vmem(F32, 3, 2, 8, 128),
            sem((7,)), sem((2,)), sem((2, 2)), sem((2, 2)),
        ],
        compiler_params=pltpu.CompilerParams(collective_id=0, has_side_effects=True, vmem_limit_bytes=48 << 20),
    )(features, norm_gain, bias_hidden, gate_logit, w_in, w_out)


def solution(mesh):
    placed = (P(("seqhi", "seqlo"), None), P(), P(), P(), P(), P())
    return jax.shard_map(body, mesh=mesh, in_specs=placed, out_specs=P(("seqhi", "seqlo"), None), check_vma=False)
```

time: 160 us -> 64 us (0.40)
  blocking collectives: 59.7 us -> 0 us
  Pallas kernels: 0 us -> 56.6 us
  waiting for transfers between devices: 46.8 us -> 0 us
  matrix products: 27 us -> 0 us
  starting transfers between devices: 16.6 us -> 0 us
  other arithmetic: 4.88 us -> 0 us
  local copies, waits for them, and re-layouts: 3.28 us -> 7.03 us
    all_to_all x2 -> x0, blocking collectives: 59.7 us -> none  [the longest x1 32.2 us: body(): lax.all_to_all(low_states, 'seqlo', split_axis=0, concat_axis=0, tiled=True)]
    pallas_call x0 -> x1, Pallas kernels: none -> 56.6 us  [body(): pl.pallas_call(kernel, out_shape=jax.ShapeDtypeStruct((rows, wide), F32),...]
    ppermute x4 -> x0, waiting for transfers between devices: 46.8 us -> none  [swapped(): return lax.ppermute(value, axis, pairs)]
    dot_general x16 -> x0, matrix products: 27 us -> none  [the longest x8 14.1 us: switch_unit(): jnp.dot(normed, w_in, precision=lax.Precision.HIGHEST, preferred_element_...]
    ppermute x4 -> x0, starting transfers between devices: 16.6 us -> none  [swapped(): return lax.ppermute(value, axis, pairs)]
    unnamed x19 -> x13, local copies, waits for them, and re-layouts: 0.75 us -> 7.03 us
    reduce_sum x16 -> x0, other arithmetic: 3.52 us -> none  [the longest x8 2.02 us: switch_unit(): center = paired - jnp.mean(paired, axis=-1, keepdims=True)]
    slice x5 -> x0, local copies, waits for them, and re-layouts: 2.17 us -> none  [the longest x1 1.08 us: params_of(): bias_hidden[layer_index]]
  transfers between devices with their start and end apart: 4 -> 0, of which waited for: 3 -> 0; matrix products, arithmetic and copies ran while one was open for 2% -> 0% of each run, Pallas kernels for 0% -> 0%
where the time goes in v1:
time: 64 us; the launch traced here: 63.6 us
  Pallas kernels  56.6 us (88%)
  local copies, waits for them, and re-layouts  7.03 us (11%)
    pallas_call x1, Pallas kernels, body(): pl.pallas_call(kernel, out_shape=jax.ShapeDtypeStruct((rows, wide), F32),...  56.6 us
    unnamed x13, local copies, waits for them, and re-layouts  7.03 us

profile of v1, /device:TPU:1, one launch (start us, length us, event | category | flops | bytes accessed | tf_op | source)
XLA Modules:
  0.0 63.6 jit_solution(13630506533039168565)
XLA Ops:
  0.0 0.0 copy-start
  0.0 1.6 %copy-done = f32[512,1024]{1,0:T(8,128)S(1)} copy-done((f32[512,1024]{1,0:T(8,128)S(1)}, f32[512,1024]{1,0:T(8,128)}, u32[]{:S(2)}) %copy-start) | copy-done | bytes 2097176
  1.6 0.0 copy-start.1
  1.6 1.6 %copy-done.1 = f32[1024,512]{1,0:T(8,128)S(1)} copy-done((f32[1024,512]{1,0:T(8,128)S(1)}, f32[1024,512]{1,0:T(8,128)}, u32[]{:S(2)}) %copy-start.1) | copy-done | bytes 2097176
  3.2 0.0 copy-start.2
  3.2 0.9 %copy-done.2 = f32[256,256]{1,0:T(8,128)S(1)} copy-done((f32[256,256]{1,0:T(8,128)S(1)}, f32[256,256]{1,0:T(8,128)}, u32[]{:S(2)}) %copy-start.2) | copy-done | bytes 262168
  4.1 0.0 copy-start.3
  4.1 0.8 %copy-done.3 = f32[8,1024]{1,0:T(8,128)S(1)} copy-done((f32[8,1024]{1,0:T(8,128)S(1)}, f32[8,1024]{1,0:T(8,128)}, u32[]{:S(2)}) %copy-start.3) | copy-done | bytes 32792
  4.9 0.0 copy-start.4
  4.9 0.7 %copy-done.4 = f32[8,512]{1,0:T(8,128)S(1)} copy-done((f32[8,512]{1,0:T(8,128)S(1)}, f32[8,512]{1,0:T(8,128)}, u32[]{:S(2)}) %copy-start.4) | copy-done | bytes 16408
  5.6 0.0 copy-start.5
  5.6 0.7 %copy-done.5 = f32[8,512]{1,0:T(8,128)S(1)} copy-done((f32[8,512]{1,0:T(8,128)S(1)}, f32[8,512]{1,0:T(8,128)}, u32[]{:S(2)}) %copy-start.5) | copy-done | bytes 16408
  6.3 56.6 %shard_map.64 = f32[256,256]{1,0:T(8,128)S(1)} custom-call(f32[256,256]{1,0:T(8,128)S(1)} %copy-done.2, f32[8,512]{1,0:T(8,128)S(1)} %copy-done.4, f32[8,1024]{1,0:T(8,128)S(1)} %copy-done.3, f32[8,512]{1,0:T(8,128)S(1)} %copy-done.5, f32[512,1024]{1,0:T(8,128)S(1)} %copy-done, f32[1024,512]{1,0:T(8,128)S(1)} %copy-done.1), custom_call_target="tpu_custom_call" | custom-call | tf_op jit(solution)/shard_map/pallas_call | solution.py:197
  62.9 0.7 %copy.8 = f32[256,256]{1,0:T(8,128)} copy(f32[256,256]{1,0:T(8,128)S(1)} %shard_map.64) | data formatting | bytes 524288
Async XLA Ops:
  0.0 1.6 %copy-start = (f32[512,1024]{1,0:T(8,128)S(1)}, f32[512,1024]{1,0:T(8,128)}, u32[]{:S(2)}) copy-start(f32[512,1024]{1,0:T(8,128)} %w_in_hbm.1) | copy-start | bytes 6291460
  1.6 1.6 %copy-start.1 = (f32[1024,512]{1,0:T(8,128)S(1)}, f32[1024,512]{1,0:T(8,128)}, u32[]{:S(2)}) copy-start(f32[1024,512]{1,0:T(8,128)} %w_out_hbm.1) | copy-start | bytes 6291460
  3.2 0.9 %copy-start.2 = (f32[256,256]{1,0:T(8,128)S(1)}, f32[256,256]{1,0:T(8,128)}, u32[]{:S(2)}) copy-start(f32[256,256]{1,0:T(8,128)} %x_hbm.1) | copy-start | bytes 786436
  4.1 0.8 %copy-start.3 = (f32[8,1024]{1,0:T(8,128)S(1)}, f32[8,1024]{1,0:T(8,128)}, u32[]{:S(2)}) copy-start(f32[8,1024]{1,0:T(8,128)} %bias_hbm.1) | copy-start | bytes 98308
  4.9 0.7 %copy-start.4 = (f32[8,512]{1,0:T(8,128)S(1)}, f32[8,512]{1,0:T(8,128)}, u32[]{:S(2)}) copy-start(f32[8,512]{1,0:T(8,128)} %gain_hbm.1) | copy-start | bytes 49156
  5.6 0.7 %copy-start.5 = (f32[8,512]{1,0:T(8,128)S(1)}, f32[8,512]{1,0:T(8,128)}, u32[]{:S(2)}) copy-start(f32[8,512]{1,0:T(8,128)} %gate_hbm.1) | copy-start | bytes 49156

commit v2 on v1

--- a/solution.py
+++ b/solution.py
@@ -1,4 +1,4 @@
-import functools
+import math
 
 import jax
 import jax.numpy as jnp
@@ -10,6 +10,8 @@
 MESH = pl.DeviceIdType.MESH
 BF, F32 = jnp.bfloat16, jnp.float32
 NORM_EPS = 1e-05
+GELU_A = (2 / math.pi) ** 0.5
+GELU_B = GELU_A * 0.044715
 Z, ZLO, X, Y = 16, 8, 4, 2
 
 
@@ -42,6 +44,12 @@
     return found
 
 
+def gelu(value):
+    inner = value * (GELU_A + GELU_B * (value * value))
+    half = 0.5 * value
+    return half + half * jnp.tanh(inner)
+
+
 def halves(value):
     high = value.astype(BF)
     return high, (value - high.astype(F32)).astype(BF)
@@ -50,8 +58,14 @@
 def product(value, weight_high, weight_low):
     rows = value.shape[0]
     high, low = halves(value)
-    both = jnp.dot(jnp.concatenate([high, low], 0), weight_high[...], preferred_element_type=F32)
-    return both[:rows] + both[rows:] + jnp.dot(high, weight_low[...], preferred_element_type=F32)
+    stacked = jnp.concatenate([high, low], 0)
+    columns = []
+    for block in range(0, weight_high.shape[0], 2):
+        tile_high = jnp.concatenate([weight_high[block], weight_high[block + 1]], -1)
+        tile_low = jnp.concatenate([weight_low[block], weight_low[block + 1]], -1)
+        both = jnp.dot(stacked, tile_high, preferred_element_type=F32)
+        columns.append(both[:rows] + both[rows:] + jnp.dot(high, tile_low, preferred_element_type=F32))
+    return jnp.concatenate(columns, -1)
 
 
 def switch(lower, upper, layer, gain, bias, gate, w_in, w_out):
@@ -61,7 +75,7 @@
     spread = (jnp.sum(lower_c * lower_c, -1, keepdims=True) + jnp.sum(upper_c * upper_c, -1, keepdims=True)) * (0.5 / wide)
     scale = lax.rsqrt(spread + NORM_EPS)
     normed = jnp.concatenate([lower_c * scale, upper_c * scale], -1) * gain[pl.ds(layer, 1), :]
-    hidden = jax.nn.gelu(product(normed, *w_in) + bias[pl.ds(layer, 1), :])
+    hidden = gelu(product(normed, *w_in) + bias[pl.ds(layer, 1), :])
     out = product(hidden, *w_out)
     kept = jax.nn.sigmoid(gate[pl.ds(layer, 1), :])
     return kept[:, :wide] * lower + out[:, :wide], kept[:, wide:] * upper + out[:, wide:]
@@ -88,7 +102,8 @@
 
     def step(index, carry):
         at = pl.ds(pl.multiple_of(index * 64, 64), 64)
-        high[at, :], low[at, :] = halves(whole[at, :])
+        for block in range(high.shape[0]):
+            high[block, at, :], low[block, at, :] = halves(whole[at, block * 128 : block * 128 + 128])
         return carry
 
     lax.fori_loop(0, rows // 64, step, 0)
@@ -101,7 +116,7 @@
 def kernel(
     x_hbm, gain_hbm, bias_hbm, gate_hbm, w_in_hbm, w_out_hbm, out,
     gain, bias, gate, w_in, w_out, in_high, in_low, out_high, out_low,
-    away, paired, mixed, points_a, points_b, spare, loads, core_sem, in_sem, out_sem,
+    away, paired, mixed, points_a, points_b, arrived, spare, loads, core_sem, in_sem, out_sem,
 ):
     hi, lo = lax.axis_index("seqhi"), lax.axis_index("seqlo")
     core = lax.rem(hi, 2)
@@ -169,23 +184,23 @@
         took(points, in_sem.at[1, which])
         butterfly(points, params, layers)
         for z_lo, to_lo, place in peers[: len(peers) - 1 + which]:
-            for part in range(2):
-                pltpu.make_async_remote_copy(
-                    src_ref=points.at[part, pl.ds(place, 1), :], dst_ref=out.at[home, pl.ds(part * 128, 128)],
-                    send_sem=out_sem.at[0, which], recv_sem=out_sem.at[1, which],
-                    device_id=(z_lo * 2 + whose, to_lo), device_id_type=MESH,
-                ).start()
+            pltpu.make_async_remote_copy(
+                src_ref=points.at[:, pl.ds(place, 1), :], dst_ref=arrived.at[:, home, :],
+                send_sem=out_sem.at[0, which], recv_sem=out_sem.at[1, which],
+                device_id=(z_lo * 2 + whose, to_lo), device_id_type=MESH,
+            ).start()
         if which == 0:
-            for part in range(2):
-                own = points.at[part, pl.ds(my_place, 1), :]
-                pltpu.make_async_copy(own, out.at[home, pl.ds(part * 128, 128)], out_sem.at[1, which]).start()
-                pltpu.make_async_copy(own, spare.at[2, part, pl.ds(0, 1), :], out_sem.at[0, which]).start()
+            own = points.at[:, pl.ds(my_place, 1), :]
+            pltpu.make_async_copy(own, arrived.at[:, home, :], out_sem.at[1, which]).start()
+            pltpu.make_async_copy(own, spare.at[2, :, pl.ds(0, 1), :], out_sem.at[0, which]).start()
 
     for which, points in enumerate((points_a, points_b)):
         took(points, in_sem.at[0, which])
         took(points, out_sem.at[0, which])
-    took(out.at[keep_at, :], out_sem.at[1, 0])
-    took(out.at[send_at, :], out_sem.at[1, 1])
+    took(arrived.at[:, keep_at, :], out_sem.at[1, 0])
+    took(arrived.at[:, send_at, :], out_sem.at[1, 1])
+    for part in range(2):
+        out[:, part * 128 : part * 128 + 128] = arrived[part]
 
 
 def body(features, norm_gain, bias_hidden, gate_logit, w_in, w_out):
@@ -202,13 +217,13 @@
         scratch_shapes=[
             vmem(F32, *norm_gain.shape), vmem(F32, *bias_hidden.shape), vmem(F32, *gate_logit.shape),
             vmem(F32, *w_in.shape), vmem(F32, *w_out.shape),
-            vmem(BF, *w_in.shape), vmem(BF, *w_in.shape), vmem(BF, *w_out.shape), vmem(BF, *w_out.shape),
+            *[vmem(BF, w.shape[1] // 128, w.shape[0], 128) for w in (w_in, w_in, w_out, w_out)],
             vmem(F32, half, wide), vmem(F32, 2, half, wide), vmem(F32, 2, 2, half, 128),
-            vmem(F32, 2, half, 128), vmem(F32, 2, half, 128), vmem(F32, 3, 2, 8, 128),
+            vmem(F32, 2, half, 128), vmem(F32, 2, half, 128), vmem(F32, 2, rows, 128), vmem(F32, 3, 2, 8, 128),
             sem((7,)), sem((2,)), sem((2, 2)), sem((2, 2)),
         ],
-        compiler_params=pltpu.CompilerParams(collective_id=0, has_side_effects=True, vmem_limit_bytes=48 << 20),
-    )(features, norm_gain, bias_hidden, gate_logit, w_in, w_out)
+        compiler_params=pltpu.CompilerParams(collective_id=0, has_side_effects=True, vmem_limit_bytes=40 << 20),
+    )(*[pltpu.with_memory_space_constraint(a, pltpu.HBM) for a in (features, norm_gain, bias_hidden, gate_logit, w_in, w_out)])
 
 
 def solution(mesh):

time: 64 us -> 56.6 us (0.88)
  local copies, waits for them, and re-layouts: 7.03 us -> 0.71 us
  Pallas kernels: 56.6 us -> 55.8 us
    unnamed x13 -> x1, local copies, waits for them, and re-layouts: 7.03 us -> 0.71 us
    pallas_call x1, Pallas kernels: 56.6 us -> 55.8 us  [body(): pl.pallas_call(kernel, out_shape=jax.ShapeDtypeStruct((rows, wide), F32),...]
where the time goes in v2:
time: 56.6 us; the launch traced here: 56.5 us
  Pallas kernels  55.8 us (99%)
  local copies, waits for them, and re-layouts  0.71 us (1%)
    pallas_call x1, Pallas kernels, body(): pl.pallas_call(kernel, out_shape=jax.ShapeDtypeStruct((rows, wide), F32),...  55.8 us

profile of v2, /device:TPU:1, one launch (start us, length us, event | category | flops | bytes accessed | tf_op | source)
XLA Modules:
  0.0 56.5 jit_solution(16497861433016325034)
XLA Ops:
  0.0 55.8 %shard_map.64 = f32[256,256]{1,0:T(8,128)S(1)} custom-call(f32[256,256]{1,0:T(8,128)} %x_hbm.1, f32[8,512]{1,0:T(8,128)} %gain_hbm.1, f32[8,1024]{1,0:T(8,128)} %bias_hbm.1, f32[8,512]{1,0:T(8,128)} %gate_hbm.1, f32[512,1024]{1,0:T(8,128)} %w_in_hbm.1, f32[1024,512]{1,0:T(8,128)} %w_out_hbm.1), custom_call_target="tpu_custom_call" | custom-call | tf_op jit(solution)/shard_map/pallas_call | solution.py:212
  55.8 0.7 %copy.8 = f32[256,256]{1,0:T(8,128)} copy(f32[256,256]{1,0:T(8,128)S(1)} %shard_map.64) | data formatting | bytes 524288

commit v3 on v2

--- a/solution.py
+++ b/solution.py
@@ -23,7 +23,7 @@
     return order
 
 
-def chips(hi, lo):
+def chips(hi, lo, turns_z, at_y=None):
     z_lo, x, z_hi, y = lax.div(hi, 2), lax.rem(lo, 4), lax.rem(lax.div(lo, 4), 2), lax.rem(lax.div(lo, 8), 2)
     block = lo - lax.rem(lo, 16)
     z = z_hi * ZLO + z_lo
@@ -31,9 +31,9 @@
     for dx in (2, 1, 3, 0):
         to = lax.rem(x + dx, X)
         along_x.append((to, lax.rem(to, 2) * 8 + lax.div(to, 2) * 4))
-    along_y = [1 - y, y]
+    along_y = [1 - y, y] if at_y is None else at_y
     found = []
-    for dz in ring_order(Z):
+    for dz in turns_z:
         to = lax.rem(z + dz, Z)
         to_hi, to_lo = lax.div(to, ZLO), lax.rem(to, ZLO)
         place_z = lax.rem(to_lo, 2) * 64 + lax.rem(lax.div(to_lo, 2), 2) * 32 + lax.div(to_lo, 4) * 16 + to_hi * 2
@@ -55,7 +55,7 @@
     return high, (value - high.astype(F32)).astype(BF)
 
 
-def product(value, weight_high, weight_low):
+def product(value, weight_high, weight_low, beside):
     rows = value.shape[0]
     high, low = halves(value)
     stacked = jnp.concatenate([high, low], 0)
@@ -65,36 +65,40 @@
         tile_low = jnp.concatenate([weight_low[block], weight_low[block + 1]], -1)
         both = jnp.dot(stacked, tile_high, preferred_element_type=F32)
         columns.append(both[:rows] + both[rows:] + jnp.dot(high, tile_low, preferred_element_type=F32))
+        beside(columns)
     return jnp.concatenate(columns, -1)
 
 
-def switch(lower, upper, layer, gain, bias, gate, w_in, w_out):
+def switch(lower, upper, layer, params, done, beside=lambda columns: None):
+    gain, bias, gate, w_in, w_out = params
     wide = lower.shape[-1]
     mean = (jnp.sum(lower, -1, keepdims=True) + jnp.sum(upper, -1, keepdims=True)) * (0.5 / wide)
     lower_c, upper_c = lower - mean, upper - mean
     spread = (jnp.sum(lower_c * lower_c, -1, keepdims=True) + jnp.sum(upper_c * upper_c, -1, keepdims=True)) * (0.5 / wide)
     scale = lax.rsqrt(spread + NORM_EPS)
     normed = jnp.concatenate([lower_c * scale, upper_c * scale], -1) * gain[pl.ds(layer, 1), :]
-    hidden = gelu(product(normed, *w_in) + bias[pl.ds(layer, 1), :])
-    out = product(hidden, *w_out)
+    hidden = gelu(product(normed, *w_in, beside) + bias[pl.ds(layer, 1), :])
     kept = jax.nn.sigmoid(gate[pl.ds(layer, 1), :])
-    return kept[:, :wide] * lower + out[:, :wide], kept[:, wide:] * upper + out[:, wide:]
-
-
-def butterfly(points, params, layers):
-    rows = points.shape[1] // 2
-
-    def step(layer, carry):
-        lower = jnp.concatenate([points[0, :rows], points[1, :rows]], -1)
-        upper = jnp.concatenate([points[0, rows:], points[1, rows:]], -1)
-        lower, upper = switch(lower, upper, layer, *params)
+
+    def finish(columns):
+        side = len(columns) - 1
+        old = (lower, upper)[side]
+        done(side, kept[:, side * wide : side * wide + wide] * old + columns[side])
+
+    product(hidden, *w_out, finish)
+
+
+def pair_layer(points, layer, params, beside=lambda columns: None, after=lambda side: None):
+    rows = points.shape[0] // 4
+    lower = jnp.concatenate([points[pl.ds(part, rows, stride=2), :] for part in range(2)], -1)
+    upper = jnp.concatenate([points[pl.ds(2 * rows + part, rows, stride=2), :] for part in range(2)], -1)
+
+    def done(side, value):
         for part in range(2):
-            lanes = slice(part * 128, part * 128 + 128)
-            points[part, pl.ds(0, rows, stride=2), :] = lower[:, lanes]
-            points[part, pl.ds(1, rows, stride=2), :] = upper[:, lanes]
-        return carry
-
-    lax.fori_loop(1, layers, step, 0)
+            points[pl.ds(2 * side + part, rows, stride=4), :] = value[:, part * 128 : part * 128 + 128]
+        after(side)
+
+    switch(lower, upper, layer, params, done, beside)
 
 
 def split_weight(whole, high, low):
@@ -107,6 +111,10 @@
         return carry
 
     lax.fori_loop(0, rows // 64, step, 0)
+
+
+def row_at(place):
+    return pl.ds(pl.multiple_of(2 * place, 2), 2)
 
 
 def took(ref, sem):
@@ -121,7 +129,7 @@
     hi, lo = lax.axis_index("seqhi"), lax.axis_index("seqlo")
     core = lax.rem(hi, 2)
     other = 1 - core
-    peers = chips(hi, lo)
+    peers = chips(hi, lo, ring_order(Z))
     my_place = peers[-1][2]
     layers = gain.shape[0]
     half = paired.shape[1]
@@ -160,47 +168,81 @@
     )
     swap.start()
     swap.wait()
-    lower, upper = switch(paired[0], paired[1], 0, *params)
-    for part in range(2):
-        lanes = slice(part * 128, part * 128 + 128)
-        mixed[0, part] = lower[:, lanes]
-        mixed[1, part] = upper[:, lanes]
+
+    def mix(side, value):
+        for part in range(2):
+            mixed[side, pl.ds(part, half, stride=2), :] = value[:, part * 128 : part * 128 + 128]
+
+    switch(paired[0], paired[1], 0, params, mix)
 
     for which, points in enumerate((points_a, points_b)):
         whose = core if which == 0 else other
         for z_lo, to_lo, place in peers[:-1]:
             pltpu.make_async_remote_copy(
-                src_ref=mixed.at[whose, :, pl.ds(place, 1), :], dst_ref=points.at[:, pl.ds(my_place, 1), :],
+                src_ref=mixed.at[whose, row_at(place), :], dst_ref=points.at[row_at(my_place), :],
                 send_sem=in_sem.at[0, which], recv_sem=in_sem.at[1, which],
                 device_id=(z_lo * 2 + core, to_lo), device_id_type=MESH,
             ).start()
-        own = mixed.at[whose, :, pl.ds(my_place, 1), :]
-        pltpu.make_async_copy(own, points.at[:, pl.ds(my_place, 1), :], in_sem.at[1, which]).start()
-        pltpu.make_async_copy(own, spare.at[which, :, pl.ds(0, 1), :], in_sem.at[0, which]).start()
-
-    home = pl.ds(core * half + my_place, 1)
-    for which, points in enumerate((points_a, points_b)):
-        whose = core if which == 0 else other
-        took(points, in_sem.at[1, which])
-        butterfly(points, params, layers)
-        for z_lo, to_lo, place in peers[: len(peers) - 1 + which]:
-            pltpu.make_async_remote_copy(
-                src_ref=points.at[:, pl.ds(place, 1), :], dst_ref=arrived.at[:, home, :],
-                send_sem=out_sem.at[0, which], recv_sem=out_sem.at[1, which],
-                device_id=(z_lo * 2 + whose, to_lo), device_id_type=MESH,
-            ).start()
-        if which == 0:
-            own = points.at[:, pl.ds(my_place, 1), :]
-            pltpu.make_async_copy(own, arrived.at[:, home, :], out_sem.at[1, which]).start()
-            pltpu.make_async_copy(own, spare.at[2, :, pl.ds(0, 1), :], out_sem.at[0, which]).start()
+        own = mixed.at[whose, row_at(my_place), :]
+        pltpu.make_async_copy(own, points.at[row_at(my_place), :], in_sem.at[1, which]).start()
+        pltpu.make_async_copy(own, spare.at[which, pl.ds(0, 2), :], in_sem.at[0, which]).start()
+
+    home = row_at(core * half + my_place)
+
+    def send_home(which, points, peer):
+        z_lo, to_lo, place = peer
+        pltpu.make_async_remote_copy(
+            src_ref=points.at[row_at(place), :], dst_ref=arrived.at[home, :],
+            send_sem=out_sem.at[0, which], recv_sem=out_sem.at[1, which],
+            device_id=(z_lo * 2 + (core if which == 0 else other), to_lo), device_id_type=MESH,
+        ).start()
+
+    took(points_a, in_sem.at[1, 0])
+
+    def alone(layer, carry):
+        pair_layer(points_a, layer, params)
+        return carry
+
+    lax.fori_loop(1, layers, alone, 0)
+    own = points_a.at[row_at(my_place), :]
+    pltpu.make_async_copy(own, arrived.at[home, :], out_sem.at[1, 0]).start()
+    pltpu.make_async_copy(own, spare.at[2, pl.ds(0, 2), :], out_sem.at[0, 0]).start()
+    for peer in chips(hi, lo, (Z - 1, 0))[:-1]:
+        send_home(0, points_a, peer)
+    took(points_b, in_sem.at[1, 1])
+
+    def both(layer, carry):
+        waiting = chips(hi, lo, (Z // 2 - 1 + layer, Z // 2 - layer))
+        share = len(waiting) // 4
+
+        def send_some(columns):
+            for peer in waiting[len(columns) * share - share : len(columns) * share]:
+                send_home(0, points_a, peer)
+
+        pair_layer(points_b, layer, params, send_some)
+        return carry
+
+    lax.fori_loop(1, layers - 1, both, 0)
+    by_y = [chips(hi, lo, ring_order(Z), (side,)) for side in range(2)]
+    last = chips(hi, lo, (Z - 2, 1))
+
+    def send_last(columns):
+        for peer in last[len(columns) * 4 - 4 : len(columns) * 4]:
+            send_home(0, points_a, peer)
+
+    def leave(side):
+        for peer in by_y[side]:
+            send_home(1, points_b, peer)
+
+    pair_layer(points_b, layers - 1, params, send_last, leave)
 
     for which, points in enumerate((points_a, points_b)):
         took(points, in_sem.at[0, which])
         took(points, out_sem.at[0, which])
-    took(arrived.at[:, keep_at, :], out_sem.at[1, 0])
-    took(arrived.at[:, send_at, :], out_sem.at[1, 1])
+    took(arrived.at[pl.ds(0, 2 * half), :], out_sem.at[1, 0])
+    took(arrived.at[pl.ds(0, 2 * half), :], out_sem.at[1, 1])
     for part in range(2):
-        out[:, part * 128 : part * 128 + 128] = arrived[part]
+        out[:, part * 128 : part * 128 + 128] = arrived[pl.ds(part, 2 * half, stride=2), :]
 
 
 def body(features, norm_gain, bias_hidden, gate_logit, w_in, w_out):
@@ -218,8 +260,8 @@
             vmem(F32, *norm_gain.shape), vmem(F32, *bias_hidden.shape), vmem(F32, *gate_logit.shape),
             vmem(F32, *w_in.shape), vmem(F32, *w_out.shape),
             *[vmem(BF, w.shape[1] // 128, w.shape[0], 128) for w in (w_in, w_in, w_out, w_out)],
-            vmem(F32, half, wide), vmem(F32, 2, half, wide), vmem(F32, 2, 2, half, 128),
-            vmem(F32, 2, half, 128), vmem(F32, 2, half, 128), vmem(F32, 2, rows, 128), vmem(F32, 3, 2, 8, 128),
+            vmem(F32, half, wide), vmem(F32, 2, half, wide), vmem(F32, 2, 2 * half, 128),
+            vmem(F32, 2 * half, 128), vmem(F32, 2 * half, 128), vmem(F32, 2 * rows, 128), vmem(F32, 3, 8, 128),
             sem((7,)), sem((2,)), sem((2, 2)), sem((2, 2)),
         ],
         compiler_params=pltpu.CompilerParams(collective_id=0, has_side_effects=True, vmem_limit_bytes=40 << 20),

time: 56.6 us -> 55.8 us (0.986)
  Pallas kernels: 55.8 us -> 54.9 us
    pallas_call x1, Pallas kernels: 55.8 us -> 54.9 us  [body(): pl.pallas_call(kernel, out_shape=jax.ShapeDtypeStruct((rows, wide), F32),...]
where the time goes in v3:
time: 55.8 us; the launch traced here: 55.6 us
  Pallas kernels  54.9 us (98%)
  local copies, waits for them, and re-layouts  0.71 us (1%)
    pallas_call x1, Pallas kernels, body(): pl.pallas_call(kernel, out_shape=jax.ShapeDtypeStruct((rows, wide), F32),...  54.9 us

profile of v3, /device:TPU:1, one launch (start us, length us, event | category | flops | bytes accessed | tf_op | source)
XLA Modules:
  0.0 55.6 jit_solution(950505816285506456)
XLA Ops:
  0.0 54.9 %shard_map.64 = f32[256,256]{1,0:T(8,128)S(1)} custom-call(f32[256,256]{1,0:T(8,128)} %x_hbm.1, f32[8,512]{1,0:T(8,128)} %gain_hbm.1, f32[8,1024]{1,0:T(8,128)} %bias_hbm.1, f32[8,512]{1,0:T(8,128)} %gate_hbm.1, f32[512,1024]{1,0:T(8,128)} %w_in_hbm.1, f32[1024,512]{1,0:T(8,128)} %w_out_hbm.1), custom_call_target="tpu_custom_call" | custom-call | tf_op jit(solution)/shard_map/pallas_call | solution.py:254
  54.9 0.7 %copy.8 = f32[256,256]{1,0:T(8,128)} copy(f32[256,256]{1,0:T(8,128)S(1)} %shard_map.64) | data formatting | bytes 524288
